TPU v7x, 256 devices: a whole 4x4x8 slice. The times are simulated.
256 devices in a mesh: tmpl: 2 (over core), row: 128 (over x, y, z).
Axes of the slice: x: 4, y: 4, z: 8, core: 2. Of those that a mesh axis runs over, the one named last changes fastest.
Arguments:
- pair_maps: bfloat16 [2, 2048, 2048, 64], P('tmpl', 'row'), may hold values from -6 to 6
- crop_tiles: int32 [2, 8], P('tmpl'), may hold values from 0 to 15, as said below
- full_length: int32 [1], replicated, may hold values from 1536 to 2048
- proj_weight: bfloat16 [2, 64, 320], replicated, may hold values from -0.75 to 0.75
- out_weight: bfloat16 [2, 64, 64], replicated, may hold values from -0.75 to 0.75
- final_weight: bfloat16 [64, 128], replicated, may hold values from -0.75 to 0.75
Outputs:
- embedding: bfloat16 [128, 1024, 1024], P(None, 'row')
Inputs may be any that keep to these rules, and one draw needn't show every extreme that they name: Each row of crop_tiles names 8 different tiles of the 16, in increasing order; its last 4 entries are the tiles 16 - 8 // 2 to 15.
All inputs are finite; a program needn't handle non-finite values.
Results may differ from a plain program's by a relative error of at most 0.014.
Values may be sent and summed in bfloat16 or wider, within the bound.
No kernel may reach another device: no remote copies, remote signals or barrier semaphores. Data moves between devices by JAX's collectives and lax.ppermute only.
A program may use at most 64 MiB of HBM per device.

v0:
```python
import jax
import jax.numpy as jnp
from jax import lax
from jax.sharding import PartitionSpec as P

CH = 64
CROP = 1024
TILE = 128
NLAYER = 2
FULL = 2048
EPSILON = 1e-05


def from_partner(value, axis, bit):
    mask = 2**bit
    pairs = [(source, source ^ mask) for source in range(lax.axis_size(axis))]
    return lax.ppermute(value, axis, pairs)


def channel_norm(values):
    center = values - jnp.mean(values, axis=0, keepdims=True)
    spread = jnp.mean(center * center, axis=0, keepdims=True)
    return center * lax.rsqrt(spread + EPSILON)


def on_device(pair_maps, crop_tiles, full_length, proj_weight, out_weight, final_weight):
    row_count = lax.axis_size("row")
    my_index = lax.axis_index("row")
    pair_local = pair_maps[0]
    crop_ids = crop_tiles[0]
    local_rows = pair_local.shape[0]
    col_width = CROP // row_count
    parts_count = max(1, row_count // CH)
    per_group = CH * parts_count // row_count
    groups = CH // per_group
    part_rows = CROP // parts_count
    steps_crop = jnp.arange(CROP, dtype=jnp.int32)
    position = crop_ids[steps_crop // TILE] * TILE + steps_crop % TILE
    usable = (position < full_length[0]).astype(jnp.float32)
    col_usable = lax.dynamic_slice_in_dim(usable, my_index * col_width, col_width)
    pair_mask = col_usable[:, None] * usable[None, :]
    columns = pair_local.reshape(local_rows, FULL // TILE, TILE, CH)[:, crop_ids]
    columns = columns.reshape(local_rows, CROP * CH)
    received = lax.all_to_all(columns, "row", split_axis=1, concat_axis=0, tiled=True)
    cropped = received.reshape(FULL // TILE, TILE, col_width * CH)[crop_ids]
    current = jnp.transpose(cropped.reshape(CROP, col_width, CH), (2, 1, 0))
    for layer_idx in range(NLAYER):
        normed_in = channel_norm(current.astype(jnp.float32)).astype(jnp.bfloat16)
        projected = jnp.einsum(
            "cd,cwi->dwi", proj_weight[layer_idx], normed_in, preferred_element_type=jnp.float32
        )
        left_proj = (jax.nn.sigmoid(projected[:CH]) * projected[CH : 2 * CH] * pair_mask).astype(
            jnp.bfloat16
        )
        right_proj = (
            jax.nn.sigmoid(projected[2 * CH : 3 * CH]) * projected[3 * CH : 4 * CH] * pair_mask
        ).astype(jnp.bfloat16)
        gate_vals = jax.nn.sigmoid(projected[4 * CH :])
        left_send = left_proj.reshape(groups, per_group, col_width, parts_count, part_rows)
        left_send = jnp.transpose(left_send, (0, 3, 1, 2, 4)).reshape(
            row_count, per_group, col_width, part_rows
        )
        right_send = right_proj.reshape(groups, per_group, col_width, parts_count, part_rows)
        right_send = jnp.transpose(right_send, (0, 3, 1, 2, 4)).reshape(
            row_count, per_group, col_width, part_rows
        )
        left_got, right_got = (
            lax.all_to_all(left_send, "row", split_axis=0, concat_axis=2, tiled=True),
            lax.all_to_all(right_send, "row", split_axis=0, concat_axis=2, tiled=True),
        )
        right_whole = right_got[0]
        partner = from_partner(right_whole, "row", 0)
        lower_side = my_index // (1 << 0) % 2 == 0
        right_whole = jnp.where(
            lower_side,
            jnp.concatenate([right_whole, partner], axis=2),
            jnp.concatenate([partner, right_whole], axis=2),
        )
        products = jnp.einsum(
            "cki,ckj->cij", left_got[0], right_whole, preferred_element_type=jnp.float32
        ).astype(jnp.bfloat16)
        back_send = jnp.transpose(
            products.reshape(per_group, part_rows, row_count, col_width), (2, 0, 3, 1)
        )
        back_got = lax.all_to_all(back_send, "row", split_axis=0, concat_axis=0, tiled=True)
        merged = back_got.reshape(groups, parts_count, per_group, col_width, part_rows)
        merged = jnp.transpose(merged, (0, 2, 3, 1, 4)).reshape(CH, col_width, CROP)
        normed_out = channel_norm(merged.astype(jnp.float32)).astype(jnp.bfloat16)
        update = jnp.einsum(
            "cd,cwi->dwi", out_weight[layer_idx], normed_out, preferred_element_type=jnp.float32
        )
        current = (current.astype(jnp.float32) + gate_vals * update).astype(jnp.bfloat16)
    normed_final = channel_norm(current.astype(jnp.float32))
    template_count = lax.axis_size("tmpl")
    summed = lax.psum(normed_final.astype(jnp.bfloat16), "tmpl").astype(jnp.float32)
    hidden = jnp.maximum(summed / template_count, 0.0).astype(jnp.bfloat16)
    result = jnp.einsum(
        "cz,cwi->zwi", final_weight, hidden, preferred_element_type=jnp.float32
    ).astype(jnp.bfloat16)
    return result


def solution(mesh):
    placed = (P("tmpl", "row", None, None), P("tmpl", None), P(), P(), P(), P())
    return jax.shard_map(
        on_device, mesh=mesh, in_specs=placed, out_specs=P(None, "row", None), check_vma=False
    )
```

profile of v0, /device:TPU:1, one launch (start us, length us, event | category | flops | bytes accessed | tf_op | source)
XLA Modules:
  0.0 438.9 jit_solution(15340569308380098732)
XLA Ops:
  6.5 0.7 fusion.91
  7.2 3.6 copy.60
  10.8 3.0 copy.41
  13.9 3.1 gather_fusion
  17.0 3.2 copy.42
  20.2 5.4 %all_to_all.19 = bf16[16,128,512]{2,1,0:T(8,128)(2,1)S(1)} reshape(bf16[16,8,128,64]{3,2,1,0:T(8,128)(2,1)} %copy.42) | data formatting | bytes 4194304 | tf_op jit(solution)/shard_map/all_to_all | solution.py:44
  25.6 2.5 copy.43
  28.1 17.0 %all-to-all-start = ((bf16[16,128,512]{2,0,1:T(8,128)(2,1)}), bf16[16,128,512]{2,0,1:T(8,128)(2,1)S(1)}, u32[]{:S(2)}, u32[]{:S(2)}) async-start(bf16[16,128,512]{2,0,1:T(8,128)(2,1)} %copy.43), calls=%async_computation | async-start | bytes 4194304 | tf_op jit(solution)/shard_map/all_to_all | solution.py:44
  45.7 0.7 fusion.96
  46.4 4.3 compare_select_fusion.1
  50.7 0.6 fusion.90
  51.5 46.3 %all-to-all-done = bf16[16,128,512]{2,0,1:T(8,128)(2,1)S(1)} async-done(((bf16[16,128,512]{2,0,1:T(8,128)(2,1)}), bf16[16,128,512]{2,0,1:T(8,128)(2,1)S(1)}, u32[]{:S(2)}, u32[]{:S(2)}) %all-to-all-start) | async-done | bytes 2097184 | tf_op jit(solution)/shard_map/all_to_all | solution.py:44
  97.8 0.6 gather_fusion.1
  98.4 1.6 copy.44
  100.0 1.7 reshape.339
  102.0 0.3 multiply_reduce_fusion
  102.6 1.6 convolution_bitcast_fusion.1
  104.3 2.8 fusion.29
  107.1 1.4 copy-done.1
  108.6 2.6 reshape.330
  111.2 3.3 copy.46
  114.5 7.3 %all-to-all-start.2 = ((bf16[128,1,8,512]{3,2,1,0:T(8,128)(2,1)}), bf16[128,1,8,512]{3,2,1,0:T(8,128)(2,1)}, u32[]{:S(2)}, u32[]{:S(2)}) async-start(bf16[128,1,8,512]{3,2,1,0:T(8,128)(2,1)} %bitcast.164), calls=%async_computation.2 | async-start | bytes 2097152 | tf_op jit(solution)/shard_map/all_to_all | solution.py:69
  121.8 1.6 reshape.327
  123.4 3.4 copy.45
  126.8 23.1 %all-to-all-done.2 = bf16[128,1,8,512]{3,2,1,0:T(8,128)(2,1)} async-done(((bf16[128,1,8,512]{3,2,1,0:T(8,128)(2,1)}), bf16[128,1,8,512]{3,2,1,0:T(8,128)(2,1)}, u32[]{:S(2)}, u32[]{:S(2)}) %all-to-all-start.2) | async-done | bytes 1048608 | tf_op jit(solution)/shard_map/all_to_all | solution.py:69
  149.9 6.2 %all-to-all-start.1 = ((bf16[128,1,8,512]{3,2,1,0:T(8,128)(2,1)}), bf16[128,1,8,512]{3,2,1,0:T(8,128)(2,1)S(1)}, u32[]{:S(2)}, u32[]{:S(2)}) async-start(bf16[128,1,8,512]{3,2,1,0:T(8,128)(2,1)} %bitcast.20), calls=%async_computation.1 | async-start | bytes 2097152 | tf_op jit(solution)/shard_map/all_to_all | solution.py:68
  156.1 0.7 collective-permute-start
  156.8 25.8 %all-to-all-done.1 = bf16[128,1,8,512]{3,2,1,0:T(8,128)(2,1)S(1)} async-done(((bf16[128,1,8,512]{3,2,1,0:T(8,128)(2,1)}), bf16[128,1,8,512]{3,2,1,0:T(8,128)(2,1)S(1)}, u32[]{:S(2)}, u32[]{:S(2)}) %all-to-all-start.1) | async-done | bytes 1048608 | tf_op jit(solution)/shard_map/all_to_all | solution.py:68
  182.6 17.1 %collective-permute-done = bf16[1,1024,512]{2,1,0:T(8,128)(2,1)} collective-permute-done((bf16[1,1024,512]{2,1,0:T(8,128)(2,1)}, bf16[1,1024,512]{2,1,0:T(8,128)(2,1)}, u32[]{:S(2)}, u32[]{:S(2)}) %collective-permute-start) | collective-permute-done | bytes 1048608 | tf_op jit(solution)/shard_map/ppermute | solution.py:17
  199.7 4.5 %fusion.66 = bf16[512,1024]{1,0:T(8,128)(2,1)} fusion(bf16[1024,512]{1,0:T(8,128)(2,1)} %bitcast.26, bf16[1024,512]{1,0:T(8,128)(2,1)} %bitcast.24, pred[]{:T(512)S(6)} %eq.9, bf16[128,1,8,512]{3,2,1,0:T(8,128)(2,1)S(1)} %all-to-all-done.1), kind=kOutput, calls=%fused_computation.95 | convolution fusion | flops 1083703296 | bytes 4194305 | tf_op jit(solution)/shard_map/cki,ckj->cij/dot_general | solution.py:79
  204.2 1.5 copy.47
  205.7 40.8 %all_to_all.62 = bf16[128,1,8,512]{3,2,1,0:T(8,128)(2,1)S(1)} all-to-all(bf16[128,1,8,512]{3,2,1,0:T(8,128)(2,1)S(1)} %bitcast.167), channel_id=1, replica_groups=mesh['tmpl'=2,'row'=128] {'row'}, dimensions={0} | all-to-all | bytes 2097152 | tf_op jit(solution)/shard_map/all_to_all | solution.py:85
  246.7 0.3 fusion.60
  247.3 0.8 copy.49
  248.1 1.5 convert_element_type.119
  249.7 2.8 convert_reduce_fusion
  252.5 0.3 fusion.4
  252.9 1.7 convolution_bitcast_fusion
  254.6 1.3 fusion.15
  255.9 2.7 copy-done.2
  258.6 1.6 reshape.336
  260.2 3.3 copy.52
  263.5 7.5 %all-to-all-start.5 = ((bf16[128,1,8,512]{3,2,1,0:T(8,128)(2,1)}), bf16[128,1,8,512]{3,2,1,0:T(8,128)(2,1)}, u32[]{:S(2)}, u32[]{:S(2)}) async-start(bf16[128,1,8,512]{3,2,1,0:T(8,128)(2,1)} %bitcast.43), calls=%async_computation.5 | async-start | bytes 2097152 | tf_op jit(solution)/shard_map/all_to_all | solution.py:69
  271.0 0.8 reshape.333
  271.8 2.1 copy.51
  273.9 23.3 %all-to-all-done.5 = bf16[128,1,8,512]{3,2,1,0:T(8,128)(2,1)} async-done(((bf16[128,1,8,512]{3,2,1,0:T(8,128)(2,1)}), bf16[128,1,8,512]{3,2,1,0:T(8,128)(2,1)}, u32[]{:S(2)}, u32[]{:S(2)}) %all-to-all-start.5) | async-done | bytes 1048608 | tf_op jit(solution)/shard_map/all_to_all | solution.py:69
  297.2 6.2 %all-to-all-start.4 = ((bf16[128,1,8,512]{3,2,1,0:T(8,128)(2,1)}), bf16[128,1,8,512]{3,2,1,0:T(8,128)(2,1)S(1)}, u32[]{:S(2)}, u32[]{:S(2)}) async-start(bf16[128,1,8,512]{3,2,1,0:T(8,128)(2,1)} %bitcast.40), calls=%async_computation.4 | async-start | bytes 2097152 | tf_op jit(solution)/shard_map/all_to_all | solution.py:68
  303.4 0.5 collective-permute-start.1
  304.0 24.5 %all-to-all-done.4 = bf16[128,1,8,512]{3,2,1,0:T(8,128)(2,1)S(1)} async-done(((bf16[128,1,8,512]{3,2,1,0:T(8,128)(2,1)}), bf16[128,1,8,512]{3,2,1,0:T(8,128)(2,1)S(1)}, u32[]{:S(2)}, u32[]{:S(2)}) %all-to-all-start.4) | async-done | bytes 1048608 | tf_op jit(solution)/shard_map/all_to_all | solution.py:68
  328.5 17.5 %collective-permute-done.1 = bf16[1,1024,512]{2,1,0:T(8,128)(2,1)S(1)} collective-permute-done((bf16[1,1024,512]{2,1,0:T(8,128)(2,1)}, bf16[1,1024,512]{2,1,0:T(8,128)(2,1)S(1)}, u32[]{:S(2)}, u32[]{:S(2)}) %collective-permute-start.1) | collective-permute-done | bytes 1048608 | tf_op jit(solution)/shard_map/ppermute | solution.py:17
  346.0 1.0 copy-done.5
  347.0 3.5 fusion.65
  350.5 0.5 copy.53
  351.0 39.6 %all_to_all.63 = bf16[128,1,8,512]{3,2,1,0:T(8,128)(2,1)S(1)} all-to-all(bf16[128,1,8,512]{3,2,1,0:T(8,128)(2,1)S(1)} %bitcast.170), channel_id=1, replica_groups=mesh['tmpl'=2,'row'=128] {'row'}, dimensions={0} | all-to-all | bytes 2097152 | tf_op jit(solution)/shard_map/all_to_all | solution.py:85
  390.7 0.3 fusion.54
  391.1 0.3 fusion.55
  391.4 0.8 copy.55
  392.2 0.8 convert_element_type.130
  393.0 2.6 convert_reduce_fusion.1
  395.6 0.3 fusion.6
  395.9 1.3 fusion.7
  397.2 29.6 %all-reduce.2.cloned.1.call-done = bf16[64,8,1024]{2,0,1:T(8,128)(2,1)} async-done(((bf16[64,8,1024]{2,0,1:T(8,128)(2,1)}), bf16[64,8,1024]{2,0,1:T(8,128)(2,1)}) %all-reduce.2.cloned.1.call-update) | async-done | bytes 1048592 | tf_op jit(solution)/shard_map/psum | solution.py:95
  426.8 2.0 convert_bitcast_fusion.2
  428.8 2.9 copy.57
  (31 shorter events, 1.5 us)
Async XLA Ops:
  6.5 420.3 %copy-start = (bf16[64,128]{1,0:T(8,128)(2,1)S(1)}, bf16[64,128]{1,0:T(8,128)(2,1)}, u32[]{:S(2)}) copy-start(bf16[64,128]{1,0:T(8,128)(2,1)} %param.11) | copy-start | bytes 49156
  28.1 17.7 %copy-start.4 = (s32[1,8]{1,0:T(1,128)S(1)}, s32[1,8]{1,0:T(1,128)}, u32[]{:S(2)}) copy-start(s32[1,8]{1,0:T(1,128)} %param.7) | copy-start | bytes 100
  28.1 69.7 %all-to-all-start = ((bf16[16,128,512]{2,0,1:T(8,128)(2,1)}), bf16[16,128,512]{2,0,1:T(8,128)(2,1)S(1)}, u32[]{:S(2)}, u32[]{:S(2)}) async-start(bf16[16,128,512]{2,0,1:T(8,128)(2,1)} %copy.43), calls=%async_computation | async-start | bytes 4194304 | tf_op jit(solution)/shard_map/all_to_all | solution.py:44
  101.7 0.9 copy-start.3
  104.3 4.3 copy-start.1
  114.5 35.4 %all-to-all-start.2 = ((bf16[128,1,8,512]{3,2,1,0:T(8,128)(2,1)}), bf16[128,1,8,512]{3,2,1,0:T(8,128)(2,1)}, u32[]{:S(2)}, u32[]{:S(2)}) async-start(bf16[128,1,8,512]{3,2,1,0:T(8,128)(2,1)} %bitcast.164), calls=%async_computation.2 | async-start | bytes 2097152 | tf_op jit(solution)/shard_map/all_to_all | solution.py:69
  149.9 32.7 %all-to-all-start.1 = ((bf16[128,1,8,512]{3,2,1,0:T(8,128)(2,1)}), bf16[128,1,8,512]{3,2,1,0:T(8,128)(2,1)S(1)}, u32[]{:S(2)}, u32[]{:S(2)}) async-start(bf16[128,1,8,512]{3,2,1,0:T(8,128)(2,1)} %bitcast.20), calls=%async_computation.1 | async-start | bytes 2097152 | tf_op jit(solution)/shard_map/all_to_all | solution.py:68
  156.1 43.6 %collective-permute-start = (bf16[1,1024,512]{2,1,0:T(8,128)(2,1)}, bf16[1,1024,512]{2,1,0:T(8,128)(2,1)}, u32[]{:S(2)}, u32[]{:S(2)}) collective-permute-start(bf16[1,1024,512]{2,1,0:T(8,128)(2,1)} %bitcast.25), channel_id=1, source_target_pairs={{0,1},{1,0},{2,3},{3,2},{4,5},{5,4},{6,7},{7,6},{8,9},{9,8},{10,11... | collective-permute-start | bytes 3145736 | tf_op jit(solution)/shard_map/ppermute | solution.py:17
  247.3 2.4 copy-start.6
  254.6 4.0 copy-start.2
  263.5 33.7 %all-to-all-start.5 = ((bf16[128,1,8,512]{3,2,1,0:T(8,128)(2,1)}), bf16[128,1,8,512]{3,2,1,0:T(8,128)(2,1)}, u32[]{:S(2)}, u32[]{:S(2)}) async-start(bf16[128,1,8,512]{3,2,1,0:T(8,128)(2,1)} %bitcast.43), calls=%async_computation.5 | async-start | bytes 2097152 | tf_op jit(solution)/shard_map/all_to_all | solution.py:69
  297.2 31.3 %all-to-all-start.4 = ((bf16[128,1,8,512]{3,2,1,0:T(8,128)(2,1)}), bf16[128,1,8,512]{3,2,1,0:T(8,128)(2,1)S(1)}, u32[]{:S(2)}, u32[]{:S(2)}) async-start(bf16[128,1,8,512]{3,2,1,0:T(8,128)(2,1)} %bitcast.40), calls=%async_computation.4 | async-start | bytes 2097152 | tf_op jit(solution)/shard_map/all_to_all | solution.py:68
  303.4 123.5 %all-reduce.2.cloned.1.call-start = ((), (), s32[]{:S(2)}) async-start(), calls=%async_computation.7 | async-start | bytes 2097152 | tf_op jit(solution)/shard_map/psum | solution.py:95
  303.4 42.6 %collective-permute-start.1 = (bf16[1,1024,512]{2,1,0:T(8,128)(2,1)}, bf16[1,1024,512]{2,1,0:T(8,128)(2,1)S(1)}, u32[]{:S(2)}, u32[]{:S(2)}) collective-permute-start(bf16[1,1024,512]{2,1,0:T(8,128)(2,1)} %bitcast.45), channel_id=1, source_target_pairs={{0,1},{1,0},{2,3},{3,2},{4,5},{5,4},{6,7},{7,6},{8,9},{9,8},{10,11... | collective-permute-start | bytes 3145736 | tf_op jit(solution)/shard_map/ppermute | solution.py:17
  346.0 1.0 copy-start.5
Sparse Core Ops, SparseCore 0:
  397.3 29.4 all-reduce.1
where the time goes:
time: 445 us; the launch traced here: 439 us
  waiting for transfers between devices  207 us (47%)
  blocking collectives  80.3 us (18%)
  local copies, waits for them, and re-layouts  58.5 us (13%)
  starting transfers between devices  45.5 us (10%)
  matrix products  18.7 us (4%)
  between operations  14.7 us (3%)
  other arithmetic  13.9 us (3%)
    all_to_all x2, blocking collectives, on_device(): lax.all_to_all(back_send, 'row', split_axis=0, concat_axis=0, tiled=True)  80.3 us
    all_to_all x2, waiting for transfers between devices, on_device(): lax.all_to_all(left_send, 'row', split_axis=0, concat_axis=2, tiled=True)  50.3 us
    all_to_all x2, waiting for transfers between devices, on_device(): lax.all_to_all(right_send, 'row', split_axis=0, concat_axis=2, tiled=True)  46.3 us
    all_to_all x1, waiting for transfers between devices, on_device(): lax.all_to_all(columns, 'row', split_axis=1, concat_axis=0, tiled=True)  46.3 us
    ppermute x2, waiting for transfers between devices, from_partner(): return lax.ppermute(value, axis, pairs)  34.6 us
    psum x1, waiting for transfers between devices, on_device(): lax.psum(normed_final.astype(jnp.bfloat16), 'tmpl').astype(jnp.float32)  29.6 us
    all_to_all x1, starting transfers between devices, on_device(): lax.all_to_all(columns, 'row', split_axis=1, concat_axis=0, tiled=True)  17 us
    all_to_all x2, starting transfers between devices, on_device(): lax.all_to_all(right_send, 'row', split_axis=0, concat_axis=2, tiled=True)  14.8 us
  transfers between devices with their start and end apart: 8, of which 8 were waited for; matrix products, arithmetic and copies ran while one was open for 3% of the time, Pallas kernels for 0%

commit v1 on v0

--- a/solution.py
+++ b/solution.py
@@ -92,7 +92,9 @@
         current = (current.astype(jnp.float32) + gate_vals * update).astype(jnp.bfloat16)
     normed_final = channel_norm(current.astype(jnp.float32))
     template_count = lax.axis_size("tmpl")
-    summed = lax.psum(normed_final.astype(jnp.bfloat16), "tmpl").astype(jnp.float32)
+    summed = jnp.sum(lax.all_gather(normed_final.astype(jnp.bfloat16), "tmpl"), axis=0).astype(
+        jnp.float32
+    )
     hidden = jnp.maximum(summed / template_count, 0.0).astype(jnp.bfloat16)
     result = jnp.einsum(
         "cz,cwi->zwi", final_weight, hidden, preferred_element_type=jnp.float32

time: 445 us -> 432 us (0.971)
  waiting for transfers between devices: 207 us -> 193 us
    psum x1 -> x0, waiting for transfers between devices: 29.6 us -> none  [on_device(): lax.psum(normed_final.astype(jnp.bfloat16), 'tmpl').astype(jnp.float32)]
    all_gather x0 -> x1, waiting for transfers between devices: none -> 15.1 us  [on_device(): lax.all_gather(normed_final.astype(jnp.bfloat16), 'tmpl')]
where the time goes in v1:
time: 432 us; the launch traced here: 425 us
  waiting for transfers between devices  193 us (45%)
  blocking collectives  80.3 us (19%)
  local copies, waits for them, and re-layouts  58.5 us (14%)
  starting transfers between devices  45.5 us (11%)
  matrix products  17.5 us (4%)
  other arithmetic  16.1 us (4%)
  between operations  14.7 us (3%)
    all_to_all x2, blocking collectives, on_device(): lax.all_to_all(back_send, 'row', split_axis=0, concat_axis=0, tiled=True)  80.3 us
    all_to_all x2, waiting for transfers between devices, on_device(): lax.all_to_all(left_send, 'row', split_axis=0, concat_axis=2, tiled=True)  50.3 us
    all_to_all x2, waiting for transfers between devices, on_device(): lax.all_to_all(right_send, 'row', split_axis=0, concat_axis=2, tiled=True)  46.3 us
    all_to_all x1, waiting for transfers between devices, on_device(): lax.all_to_all(columns, 'row', split_axis=1, concat_axis=0, tiled=True)  46.3 us
    ppermute x2, waiting for transfers between devices, from_partner(): return lax.ppermute(value, axis, pairs)  34.6 us
    all_to_all x1, starting transfers between devices, on_device(): lax.all_to_all(columns, 'row', split_axis=1, concat_axis=0, tiled=True)  17 us
    all_gather x1, waiting for transfers between devices, on_device(): lax.all_gather(normed_final.astype(jnp.bfloat16), 'tmpl')  15.1 us
    all_to_all x2, starting transfers between devices, on_device(): lax.all_to_all(right_send, 'row', split_axis=0, concat_axis=2, tiled=True)  14.8 us
  transfers between devices with their start and end apart: 8, of which 8 were waited for; matrix products, arithmetic and copies ran while one was open for 3% of the time, Pallas kernels for 0%

profile of v1, /device:TPU:1, one launch (start us, length us, event | category | flops | bytes accessed | tf_op | source)
XLA Modules:
  0.0 425.4 jit_solution(4491461182885584837)
XLA Ops:
  6.5 0.7 fusion.91
  7.2 3.6 copy.60
  10.8 3.0 copy.41
  13.9 3.1 gather_fusion
  17.0 3.2 copy.42
  20.2 5.4 %all_to_all.19 = bf16[16,128,512]{2,1,0:T(8,128)(2,1)S(1)} reshape(bf16[16,8,128,64]{3,2,1,0:T(8,128)(2,1)} %copy.42) | data formatting | bytes 4194304 | tf_op jit(solution)/shard_map/all_to_all | solution.py:44
  25.6 2.5 copy.43
  28.1 17.0 %all-to-all-start = ((bf16[16,128,512]{2,0,1:T(8,128)(2,1)}), bf16[16,128,512]{2,0,1:T(8,128)(2,1)S(1)}, u32[]{:S(2)}, u32[]{:S(2)}) async-start(bf16[16,128,512]{2,0,1:T(8,128)(2,1)} %copy.43), calls=%async_computation | async-start | bytes 4194304 | tf_op jit(solution)/shard_map/all_to_all | solution.py:44
  45.7 0.7 fusion.96
  46.4 4.3 %compare_select_fusion.1 = s32[1024,1]{0,1:T(1,128)S(1)} fusion(s32[]{:T(128)} %bitcast.10, s32[]{:T(128)} %bitcast.11, s32[]{:T(128)} %bitcast.12, s32[]{:T(128)} %bitcast.13, s32[]{:T(128)} %bitcast.14, s32[]{:T(128)} %bitcast.16, s32[]{:T(128)} %bitcast.15), kind=kLoop, calls=%fused_computation.126 | loop fusion | flops 23552 | bytes 4124 | tf_op jit(solution)/shard_map/gather | solution.py:38
  50.7 0.6 fusion.90
  51.5 46.3 %all-to-all-done = bf16[16,128,512]{2,0,1:T(8,128)(2,1)S(1)} async-done(((bf16[16,128,512]{2,0,1:T(8,128)(2,1)}), bf16[16,128,512]{2,0,1:T(8,128)(2,1)S(1)}, u32[]{:S(2)}, u32[]{:S(2)}) %all-to-all-start) | async-done | bytes 2097184 | tf_op jit(solution)/shard_map/all_to_all | solution.py:44
  97.8 0.6 gather_fusion.1
  98.4 1.6 copy.44
  100.0 1.7 reshape.339
  102.0 0.3 multiply_reduce_fusion
  102.6 1.6 convolution_bitcast_fusion.1
  104.3 2.8 fusion.29
  107.1 1.4 copy-done.1
  108.6 2.6 reshape.330
  111.2 3.3 copy.46
  114.5 7.3 %all-to-all-start.2 = ((bf16[128,1,8,512]{3,2,1,0:T(8,128)(2,1)}), bf16[128,1,8,512]{3,2,1,0:T(8,128)(2,1)}, u32[]{:S(2)}, u32[]{:S(2)}) async-start(bf16[128,1,8,512]{3,2,1,0:T(8,128)(2,1)} %bitcast.165), calls=%async_computation.2 | async-start | bytes 2097152 | tf_op jit(solution)/shard_map/all_to_all | solution.py:69
  121.8 1.6 reshape.327
  123.4 3.4 copy.45
  126.8 23.1 %all-to-all-done.2 = bf16[128,1,8,512]{3,2,1,0:T(8,128)(2,1)} async-done(((bf16[128,1,8,512]{3,2,1,0:T(8,128)(2,1)}), bf16[128,1,8,512]{3,2,1,0:T(8,128)(2,1)}, u32[]{:S(2)}, u32[]{:S(2)}) %all-to-all-start.2) | async-done | bytes 1048608 | tf_op jit(solution)/shard_map/all_to_all | solution.py:69
  149.9 6.2 %all-to-all-start.1 = ((bf16[128,1,8,512]{3,2,1,0:T(8,128)(2,1)}), bf16[128,1,8,512]{3,2,1,0:T(8,128)(2,1)S(1)}, u32[]{:S(2)}, u32[]{:S(2)}) async-start(bf16[128,1,8,512]{3,2,1,0:T(8,128)(2,1)} %bitcast.20), calls=%async_computation.1 | async-start | bytes 2097152 | tf_op jit(solution)/shard_map/all_to_all | solution.py:68
  156.1 0.7 collective-permute-start
  156.8 25.8 %all-to-all-done.1 = bf16[128,1,8,512]{3,2,1,0:T(8,128)(2,1)S(1)} async-done(((bf16[128,1,8,512]{3,2,1,0:T(8,128)(2,1)}), bf16[128,1,8,512]{3,2,1,0:T(8,128)(2,1)S(1)}, u32[]{:S(2)}, u32[]{:S(2)}) %all-to-all-start.1) | async-done | bytes 1048608 | tf_op jit(solution)/shard_map/all_to_all | solution.py:68
  182.6 17.1 %collective-permute-done = bf16[1,1024,512]{2,1,0:T(8,128)(2,1)} collective-permute-done((bf16[1,1024,512]{2,1,0:T(8,128)(2,1)}, bf16[1,1024,512]{2,1,0:T(8,128)(2,1)}, u32[]{:S(2)}, u32[]{:S(2)}) %collective-permute-start) | collective-permute-done | bytes 1048608 | tf_op jit(solution)/shard_map/ppermute | solution.py:17
  199.7 4.5 %fusion.66 = bf16[512,1024]{1,0:T(8,128)(2,1)} fusion(bf16[1024,512]{1,0:T(8,128)(2,1)} %bitcast.26, bf16[1024,512]{1,0:T(8,128)(2,1)} %bitcast.24, pred[]{:T(512)S(6)} %eq.9, bf16[128,1,8,512]{3,2,1,0:T(8,128)(2,1)S(1)} %all-to-all-done.1), kind=kOutput, calls=%fused_computation.95 | convolution fusion | flops 1083703296 | bytes 4194305 | tf_op jit(solution)/shard_map/cki,ckj->cij/dot_general | solution.py:79
  204.2 1.5 copy.47
  205.7 40.8 %all_to_all.62 = bf16[128,1,8,512]{3,2,1,0:T(8,128)(2,1)S(1)} all-to-all(bf16[128,1,8,512]{3,2,1,0:T(8,128)(2,1)S(1)} %bitcast.168), channel_id=1, replica_groups=mesh['tmpl'=2,'row'=128] {'row'}, dimensions={0} | all-to-all | bytes 2097152 | tf_op jit(solution)/shard_map/all_to_all | solution.py:85
  246.7 0.3 fusion.60
  247.3 0.8 copy.49
  248.1 1.5 convert_element_type.121
  249.7 2.8 convert_reduce_fusion
  252.5 0.3 fusion.4
  252.9 1.7 convolution_bitcast_fusion
  254.6 1.3 fusion.15
  255.9 2.7 copy-done.2
  258.6 1.6 reshape.336
  260.2 3.3 copy.52
  263.5 7.5 %all-to-all-start.5 = ((bf16[128,1,8,512]{3,2,1,0:T(8,128)(2,1)}), bf16[128,1,8,512]{3,2,1,0:T(8,128)(2,1)}, u32[]{:S(2)}, u32[]{:S(2)}) async-start(bf16[128,1,8,512]{3,2,1,0:T(8,128)(2,1)} %bitcast.43), calls=%async_computation.5 | async-start | bytes 2097152 | tf_op jit(solution)/shard_map/all_to_all | solution.py:69
  271.0 0.8 reshape.333
  271.8 2.1 copy.51
  273.9 23.3 %all-to-all-done.5 = bf16[128,1,8,512]{3,2,1,0:T(8,128)(2,1)} async-done(((bf16[128,1,8,512]{3,2,1,0:T(8,128)(2,1)}), bf16[128,1,8,512]{3,2,1,0:T(8,128)(2,1)}, u32[]{:S(2)}, u32[]{:S(2)}) %all-to-all-start.5) | async-done | bytes 1048608 | tf_op jit(solution)/shard_map/all_to_all | solution.py:69
  297.2 6.2 %all-to-all-start.4 = ((bf16[128,1,8,512]{3,2,1,0:T(8,128)(2,1)}), bf16[128,1,8,512]{3,2,1,0:T(8,128)(2,1)S(1)}, u32[]{:S(2)}, u32[]{:S(2)}) async-start(bf16[128,1,8,512]{3,2,1,0:T(8,128)(2,1)} %bitcast.40), calls=%async_computation.4 | async-start | bytes 2097152 | tf_op jit(solution)/shard_map/all_to_all | solution.py:68
  303.4 0.5 collective-permute-start.1
  304.0 24.5 %all-to-all-done.4 = bf16[128,1,8,512]{3,2,1,0:T(8,128)(2,1)S(1)} async-done(((bf16[128,1,8,512]{3,2,1,0:T(8,128)(2,1)}), bf16[128,1,8,512]{3,2,1,0:T(8,128)(2,1)S(1)}, u32[]{:S(2)}, u32[]{:S(2)}) %all-to-all-start.4) | async-done | bytes 1048608 | tf_op jit(solution)/shard_map/all_to_all | solution.py:68
  328.5 17.5 %collective-permute-done.1 = bf16[1,1024,512]{2,1,0:T(8,128)(2,1)S(1)} collective-permute-done((bf16[1,1024,512]{2,1,0:T(8,128)(2,1)}, bf16[1,1024,512]{2,1,0:T(8,128)(2,1)S(1)}, u32[]{:S(2)}, u32[]{:S(2)}) %collective-permute-start.1) | collective-permute-done | bytes 1048608 | tf_op jit(solution)/shard_map/ppermute | solution.py:17
  346.0 1.0 copy-done.5
  347.0 3.5 fusion.65
  350.5 0.5 copy.53
  351.0 39.6 %all_to_all.63 = bf16[128,1,8,512]{3,2,1,0:T(8,128)(2,1)S(1)} all-to-all(bf16[128,1,8,512]{3,2,1,0:T(8,128)(2,1)S(1)} %bitcast.171), channel_id=1, replica_groups=mesh['tmpl'=2,'row'=128] {'row'}, dimensions={0} | all-to-all | bytes 2097152 | tf_op jit(solution)/shard_map/all_to_all | solution.py:85
  390.7 0.3 fusion.54
  391.4 0.8 copy.55
  392.2 0.8 convert_element_type.132
  393.0 2.6 convert_reduce_fusion.1
  395.6 0.3 fusion.6
  395.9 1.3 fusion.7
  397.2 15.1 %all-gather.3.cloned.1.call-done = bf16[128,8,1024]{2,0,1:T(8,128)(2,1)} async-done(((bf16[64,8,1024]{2,0,1:T(8,128)(2,1)}), bf16[128,8,1024]{2,0,1:T(8,128)(2,1)}) %all-gather.3.cloned.1.call-update) | async-done | bytes 2097168 | tf_op jit(solution)/shard_map/all_gather | solution.py:95
  412.4 2.2 reduce_sum.112
  414.6 0.8 convert_bitcast_fusion.2
  415.4 2.9 copy.57
  (32 shorter events, 1.8 us)
Async XLA Ops:
  6.5 408.0 %copy-start = (bf16[64,128]{1,0:T(8,128)(2,1)S(1)}, bf16[64,128]{1,0:T(8,128)(2,1)}, u32[]{:S(2)}) copy-start(bf16[64,128]{1,0:T(8,128)(2,1)} %param.11) | copy-start | bytes 49156
  28.1 17.7 %copy-start.4 = (s32[1,8]{1,0:T(1,128)S(1)}, s32[1,8]{1,0:T(1,128)}, u32[]{:S(2)}) copy-start(s32[1,8]{1,0:T(1,128)} %param.7) | copy-start | bytes 100
  28.1 69.7 %all-to-all-start = ((bf16[16,128,512]{2,0,1:T(8,128)(2,1)}), bf16[16,128,512]{2,0,1:T(8,128)(2,1)S(1)}, u32[]{:S(2)}, u32[]{:S(2)}) async-start(bf16[16,128,512]{2,0,1:T(8,128)(2,1)} %copy.43), calls=%async_computation | async-start | bytes 4194304 | tf_op jit(solution)/shard_map/all_to_all | solution.py:44
  101.7 0.9 copy-start.3
  104.3 4.3 %copy-start.1 = (f32[320,8,1024]{2,0,1:T(8,128)}, f32[320,8,1024]{2,0,1:T(8,128)S(1)}, u32[]{:S(2)}) copy-start(f32[320,8,1024]{2,0,1:T(8,128)S(1)} %convolution_bitcast_fusion.1) | copy-start | bytes 31457284
  114.5 35.4 %all-to-all-start.2 = ((bf16[128,1,8,512]{3,2,1,0:T(8,128)(2,1)}), bf16[128,1,8,512]{3,2,1,0:T(8,128)(2,1)}, u32[]{:S(2)}, u32[]{:S(2)}) async-start(bf16[128,1,8,512]{3,2,1,0:T(8,128)(2,1)} %bitcast.165), calls=%async_computation.2 | async-start | bytes 2097152 | tf_op jit(solution)/shard_map/all_to_all | solution.py:69
  149.9 32.7 %all-to-all-start.1 = ((bf16[128,1,8,512]{3,2,1,0:T(8,128)(2,1)}), bf16[128,1,8,512]{3,2,1,0:T(8,128)(2,1)S(1)}, u32[]{:S(2)}, u32[]{:S(2)}) async-start(bf16[128,1,8,512]{3,2,1,0:T(8,128)(2,1)} %bitcast.20), calls=%async_computation.1 | async-start | bytes 2097152 | tf_op jit(solution)/shard_map/all_to_all | solution.py:68
  156.1 43.6 %collective-permute-start = (bf16[1,1024,512]{2,1,0:T(8,128)(2,1)}, bf16[1,1024,512]{2,1,0:T(8,128)(2,1)}, u32[]{:S(2)}, u32[]{:S(2)}) collective-permute-start(bf16[1,1024,512]{2,1,0:T(8,128)(2,1)} %bitcast.25), channel_id=1, source_target_pairs={{0,1},{1,0},{2,3},{3,2},{4,5},{5,4},{6,7},{7,6},{8,9},{9,8},{10,11... | collective-permute-start | bytes 3145736 | tf_op jit(solution)/shard_map/ppermute | solution.py:17
  247.3 2.4 copy-start.6
  254.6 4.0 copy-start.2
  263.5 33.7 %all-to-all-start.5 = ((bf16[128,1,8,512]{3,2,1,0:T(8,128)(2,1)}), bf16[128,1,8,512]{3,2,1,0:T(8,128)(2,1)}, u32[]{:S(2)}, u32[]{:S(2)}) async-start(bf16[128,1,8,512]{3,2,1,0:T(8,128)(2,1)} %bitcast.43), calls=%async_computation.5 | async-start | bytes 2097152 | tf_op jit(solution)/shard_map/all_to_all | solution.py:69
  297.2 31.3 %all-to-all-start.4 = ((bf16[128,1,8,512]{3,2,1,0:T(8,128)(2,1)}), bf16[128,1,8,512]{3,2,1,0:T(8,128)(2,1)S(1)}, u32[]{:S(2)}, u32[]{:S(2)}) async-start(bf16[128,1,8,512]{3,2,1,0:T(8,128)(2,1)} %bitcast.40), calls=%async_computation.4 | async-start | bytes 2097152 | tf_op jit(solution)/shard_map/all_to_all | solution.py:68
  303.4 109.0 %all-gather.3.cloned.1.call-start = ((), (), s32[]{:S(2)}) async-start(), calls=%async_computation.7 | async-start | bytes 3145728 | tf_op jit(solution)/shard_map/all_gather | solution.py:95
  303.4 42.6 %collective-permute-start.1 = (bf16[1,1024,512]{2,1,0:T(8,128)(2,1)}, bf16[1,1024,512]{2,1,0:T(8,128)(2,1)S(1)}, u32[]{:S(2)}, u32[]{:S(2)}) collective-permute-start(bf16[1,1024,512]{2,1,0:T(8,128)(2,1)} %bitcast.45), channel_id=1, source_target_pairs={{0,1},{1,0},{2,3},{3,2},{4,5},{5,4},{6,7},{7,6},{8,9},{9,8},{10,11... | collective-permute-start | bytes 3145736 | tf_op jit(solution)/shard_map/ppermute | solution.py:17
  346.0 1.0 copy-start.5
Sparse Core Ops, SparseCore 0:
  397.3 14.9 all-gather.2
